TPU v7x, 256 devices: a whole 4x4x8 slice. The times are simulated.
256 devices in a mesh: grp: 4 (over y), wide: 64 (over z, x, core).
Axes of the slice: x: 4, y: 4, z: 8, core: 2. Of those that a mesh axis runs over, the one named last changes fastest.
Arguments:
- tiles: bfloat16 [12288, 256, 256], P(('grp', 'wide')), may hold values from -0.59765625 to 0.59765625
- contraction: int32 [12288], P(('grp', 'wide')), may hold values from 0 to 15
- row_tile: int32 [12288], P(('grp', 'wide')), may hold values from 0 to 255, as said below
- owner_map: int32 [256], replicated, may hold values from 0 to 255, as said below
- panel: bfloat16 [4096, 768], P('grp'), may hold values from -0.5390625 to 0.5390625
Outputs:
- column_block: float32 [65536, 768], P('wide')
Inputs may be any that keep to these rules, and one draw needn't show every extreme that they name: `row_tile`: every row tile's owner is owner_map // 4; among the 48 contributions of one device at most 2 have row tiles of one owner, and on every device some owner gets exactly 2. `owner_map`: A permutation of the row tiles.
All inputs are finite; a program needn't handle non-finite values.
Results may differ from a plain program's by a relative error of at most 0.0003.
Values may be sent and summed in bfloat16 or wider, within the bound.
A program may use at most 192 MiB of HBM per device.

v0:
```python
import math
import jax
import jax.numpy as jnp
from jax import lax
from jax.sharding import PartitionSpec as P


def place_slots(row_ids, owner_map, out_dev):
    table_ids = jnp.arange(owner_map.shape[0], dtype=jnp.int32)
    position = jnp.sum(jnp.where(row_ids[..., None] == table_ids, owner_map, 0), axis=-1)
    target = position // out_dev
    serial = jnp.arange(row_ids.shape[-1], dtype=jnp.int32)
    earlier = (target[..., :, None] == target[..., None, :]) & (serial[:, None] > serial[None, :])
    ranking = jnp.sum(earlier.astype(jnp.int32), axis=-1)
    return (position % out_dev, target, ranking)


def add_products(summed, arrived, slot_labels, panel_tiles):
    slot_count = arrived.shape[0]
    block_rows = math.gcd(slot_count, 32)
    out_dev = summed.shape[0]
    local_ids = jnp.arange(out_dev, dtype=jnp.int32)

    def one_block(which_block, running, source_tiles, source_labels):
        part_tiles = lax.dynamic_slice_in_dim(source_tiles, which_block * block_rows, block_rows, 0)
        part_labels = lax.dynamic_slice_in_dim(
            source_labels, which_block * block_rows, block_rows, 0
        )
        chosen = jnp.take(panel_tiles, part_labels[:, 1], axis=0)
        products = jnp.einsum(
            "sab,sbc->sac", part_tiles, chosen, preferred_element_type=jnp.float32
        )
        row_hits = (part_labels[:, 0][:, None] == local_ids[None, :]).astype(jnp.float32)
        return running + jnp.einsum(
            "sr,sac->rac", row_hits, products, precision=lax.Precision.HIGHEST
        )

    return lax.fori_loop(
        0,
        slot_count // block_rows,
        lambda which_block, running: one_block(which_block, running, arrived, slot_labels),
        summed,
    )


def per_device(tiles, contraction, row_tile, owner_map, panel):
    wide_count = lax.axis_size("wide")
    tile_dev = tiles.shape[0]
    tile_side = tiles.shape[1]
    out_dev = owner_map.shape[0] // wide_count
    most_slots = tile_dev * 8 // (3 * wide_count)
    slot_total = wide_count * most_slots
    local_row, target, ranking = place_slots(row_tile, owner_map, out_dev)
    slot_index = target * most_slots + ranking
    outgoing = jnp.zeros((slot_total, tile_side, tile_side), tiles.dtype).at[slot_index].set(tiles)
    all_rows, all_contraction = (
        lax.all_gather(row_tile, "wide", axis=0, tiled=True),
        lax.all_gather(contraction, "wide", axis=0, tiled=True),
    )
    all_rows = all_rows.reshape(wide_count, tile_dev)
    all_contraction = all_contraction.reshape(wide_count, tile_dev)
    source_local, source_target, source_rank = place_slots(all_rows, owner_map, out_dev)
    source_ids = jnp.arange(wide_count, dtype=jnp.int32)
    mine = source_target == lax.axis_index("wide")
    arrive_index = jnp.where(mine, source_ids[:, None] * most_slots + source_rank, slot_total)
    label_pairs = jnp.stack([source_local, all_contraction], axis=-1).reshape(
        wide_count * tile_dev, 2
    )
    vacant_label = jnp.stack(
        [jnp.full((slot_total,), out_dev, jnp.int32), jnp.zeros((slot_total,), jnp.int32)], axis=1
    )
    arrived_labels = vacant_label.at[arrive_index.reshape(-1)].set(label_pairs, mode="drop")
    gathered = lax.all_gather(panel, "grp", axis=0, tiled=True)
    panel_tiles = gathered.reshape(gathered.shape[0] // tile_side, tile_side, gathered.shape[1])
    summed = jnp.zeros((out_dev, tile_side, gathered.shape[1]), jnp.float32)
    arrived = lax.all_to_all(outgoing, "wide", split_axis=0, concat_axis=0, tiled=True)
    summed = add_products(summed, arrived, arrived_labels, panel_tiles)
    summed = lax.psum(summed, "grp")
    return summed.reshape(out_dev * tile_side, gathered.shape[1])


def solution(mesh):
    return jax.shard_map(
        per_device,
        mesh=mesh,
        in_specs=(
            P(("grp", "wide"), None, None),
            P(("grp", "wide")),
            P(("grp", "wide")),
            P(),
            P("grp", None),
        ),
        out_specs=P("wide", None),
        check_vma=False,
    )
```

profile of v0, /device:TPU:1, one launch (start us, length us, event | category | flops | bytes accessed | tf_op | source)
XLA Modules:
  0.0 973.6 jit_solution(2914574177467141061)
XLA Ops:
  6.5 0.9 select_reduce_fusion.1
  7.4 0.2 convert_reduce_fusion.1
  7.6 5.9 broadcast_in_dim.68
  13.5 16.8 %scatter_fusion.1 = bf16[128,256,256]{2,1,0:T(8,128)(2,1)} fusion(bf16[128,256,256]{2,1,0:T(8,128)(2,1)} %broadcast_in_dim.68, s32[48]{0:T(128)S(1)} %fusion.19, bf16[48,256,256]{2,1,0:T(8,128)(2,1)} %param.7), kind=kCustom, calls=%fused_computation.2 | custom fusion | bytes 18874560 | tf_op jit(solution)/shard_map/scatter | solution.py:55
  30.4 13.3 %all-to-all-start = ((bf16[128,256,256]{2,1,0:T(8,128)(2,1)}), bf16[128,256,256]{2,1,0:T(8,128)(2,1)}, u32[]{:S(2)}, u32[]{:S(2)}) async-start(bf16[128,256,256]{2,1,0:T(8,128)(2,1)} %scatter_fusion.1), calls=%async_computation | async-start | bytes 33554432 | tf_op jit(solution)/shard_map/all_to_all | solution.py:76
  43.6 0.0 copy-start
  43.6 0.0 all-gather.2.cloned.1.call-start
  43.7 0.7 all-gather.2.cloned.1.call-update
  44.4 0.0 all-reduce.5.cloned.1.call-start
  44.5 0.0 copy-done.4
  44.5 0.6 dynamic-slice
  45.7 0.3 dynamic-update-slice
  46.0 0.3 dynamic-update-slice.1
  46.3 588.5 %all-reduce.2 = (s32[3072]{0:T(1024)S(1)}, s32[3072]{0:T(1024)S(1)}) all-reduce(s32[3072]{0:T(1024)S(1)} %dynamic-update-slice, s32[3072]{0:T(1024)S(1)} %dynamic-update-slice.1), channel_id=1, replica_groups=mesh['grp'=4,'wide'=64] {'wide'}, use_global_device_ids=true, to_apply=%add | all-reduce | flops 6144 | bytes 49152
  634.8 0.1 eq.107
  634.9 1.7 select_reduce_fusion
  636.6 0.1 reduce_sum.43
  636.7 0.1 copy.11
  636.8 0.5 convert_reduce_fusion
  637.3 0.1 copy.13
  637.4 0.1 add.152
  637.5 0.1 and_select_fusion
  637.6 1.7 copy.14
  639.3 0.0 copy-done
  639.3 8.5 scatter_fusion
  647.8 0.1 copy.15
  647.9 0.0 all-to-all-done
  647.9 231.6 %while.14 = (s32[]{:T(128)}, f32[4,256,768]{2,0,1:T(4,128)S(1)}, s32[128,2]{0,1:T(2,128)S(1)}, bf16[128,256,256]{2,1,0:T(8,128)(2,1)}, bf16[16,256,768]{2,1,0:T(...) while((s32[]{:T(128)}, f32[4,256,768]{2,0,1:T(4,128)S(1)}, ...), condition=%wide.region_7.8_spmd.clone, body=%wide.region_6.7_spmd.clone.sunk | while | flops 3531081216 | bytes 98572000 | solution.py:38
  648.1 0.1 constant_dynamic-slice_fusion.2
  648.2 9.4 gather_fusion
  657.5 17.7 %fusion.29 = f32[32,256,768]{2,1,0:T(8,128)} fusion(bf16[32,256,768]{2,1,0:T(8,128)(2,1)} %gather_fusion, pred[32]{0:T(512)(128)(4,1)S(1)} %and_bitcast_fusion.2, bf16[128,256,256]{2,1,0:T(8,128)(2,1)} %get-tuple-element.217, s32[]{:T(128)S(6)} %select_n.171), kind=kOutput, calls=%fused_computation.6.clone.1 | convolution fusion | flops 3227516928 | bytes 41943076 | tf_op jit(solution)/shard_map/while/body/eval_jaxpr/sab,sbc->sac/dot_general | solution.py:30
  675.2 30.7 %select_add_fusion.2 = f32[4,256,768]{2,0,1:T(4,128)S(1)} fusion(f32[4,256,768]{2,0,1:T(4,128)S(1)} %get-tuple-element.206, pred[]{:T(512)S(6)} %compare.49, f32[32,256,768]{2,1,0:T(8,128)} %fusion.29, s32[32]{0:T(128)S(1)} %get-tuple-element.195), kind=kOutput, calls=%fused_computation.11.clone.1 | convolution fusion | flops 303562880 | bytes 31457408 | tf_op jit(solution)/shard_map/while/body/eval_jaxpr/sr,sac->rac/dot_general | solution.py:34
  706.0 0.1 constant_dynamic-slice_fusion.2
  706.1 9.3 gather_fusion
  715.4 17.7 %fusion.29 = f32[32,256,768]{2,1,0:T(8,128)} fusion(bf16[32,256,768]{2,1,0:T(8,128)(2,1)} %gather_fusion, pred[32]{0:T(512)(128)(4,1)S(1)} %and_bitcast_fusion.2, bf16[128,256,256]{2,1,0:T(8,128)(2,1)} %get-tuple-element.217, s32[]{:T(128)S(6)} %select_n.171), kind=kOutput, calls=%fused_computation.6.clone.1 | convolution fusion | flops 3227516928 | bytes 41943076 | tf_op jit(solution)/shard_map/while/body/eval_jaxpr/sab,sbc->sac/dot_general | solution.py:30
  733.1 30.7 %select_add_fusion.2 = f32[4,256,768]{2,0,1:T(4,128)S(1)} fusion(f32[4,256,768]{2,0,1:T(4,128)S(1)} %get-tuple-element.206, pred[]{:T(512)S(6)} %compare.49, f32[32,256,768]{2,1,0:T(8,128)} %fusion.29, s32[32]{0:T(128)S(1)} %get-tuple-element.195), kind=kOutput, calls=%fused_computation.11.clone.1 | convolution fusion | flops 303562880 | bytes 31457408 | tf_op jit(solution)/shard_map/while/body/eval_jaxpr/sr,sac->rac/dot_general | solution.py:34
  763.8 0.1 constant_dynamic-slice_fusion.2
  763.9 9.3 gather_fusion
  773.2 17.7 %fusion.29 = f32[32,256,768]{2,1,0:T(8,128)} fusion(bf16[32,256,768]{2,1,0:T(8,128)(2,1)} %gather_fusion, pred[32]{0:T(512)(128)(4,1)S(1)} %and_bitcast_fusion.2, bf16[128,256,256]{2,1,0:T(8,128)(2,1)} %get-tuple-element.217, s32[]{:T(128)S(6)} %select_n.171), kind=kOutput, calls=%fused_computation.6.clone.1 | convolution fusion | flops 3227516928 | bytes 41943076 | tf_op jit(solution)/shard_map/while/body/eval_jaxpr/sab,sbc->sac/dot_general | solution.py:30
  790.9 30.7 %select_add_fusion.2 = f32[4,256,768]{2,0,1:T(4,128)S(1)} fusion(f32[4,256,768]{2,0,1:T(4,128)S(1)} %get-tuple-element.206, pred[]{:T(512)S(6)} %compare.49, f32[32,256,768]{2,1,0:T(8,128)} %fusion.29, s32[32]{0:T(128)S(1)} %get-tuple-element.195), kind=kOutput, calls=%fused_computation.11.clone.1 | convolution fusion | flops 303562880 | bytes 31457408 | tf_op jit(solution)/shard_map/while/body/eval_jaxpr/sr,sac->rac/dot_general | solution.py:34
  821.7 0.1 constant_dynamic-slice_fusion.2
  821.8 9.2 gather_fusion
  831.0 17.7 %fusion.29 = f32[32,256,768]{2,1,0:T(8,128)} fusion(bf16[32,256,768]{2,1,0:T(8,128)(2,1)} %gather_fusion, pred[32]{0:T(512)(128)(4,1)S(1)} %and_bitcast_fusion.2, bf16[128,256,256]{2,1,0:T(8,128)(2,1)} %get-tuple-element.217, s32[]{:T(128)S(6)} %select_n.171), kind=kOutput, calls=%fused_computation.6.clone.1 | convolution fusion | flops 3227516928 | bytes 41943076 | tf_op jit(solution)/shard_map/while/body/eval_jaxpr/sab,sbc->sac/dot_general | solution.py:30
  848.7 30.7 %select_add_fusion.2 = f32[4,256,768]{2,0,1:T(4,128)S(1)} fusion(f32[4,256,768]{2,0,1:T(4,128)S(1)} %get-tuple-element.206, pred[]{:T(512)S(6)} %compare.49, f32[32,256,768]{2,1,0:T(8,128)} %fusion.29, s32[32]{0:T(128)S(1)} %get-tuple-element.195), kind=kOutput, calls=%fused_computation.11.clone.1 | convolution fusion | flops 303562880 | bytes 31457408 | tf_op jit(solution)/shard_map/while/body/eval_jaxpr/sr,sac->rac/dot_general | solution.py:34
  879.5 2.2 copy.16
  881.7 0.0 all-reduce.5.cloned.1.call-update
  881.7 81.3 %all-reduce.5.cloned.1.call-done = f32[1024,768]{1,0:T(8,128)} async-done(((f32[1024,768]{1,0:T(8,128)}), f32[1024,768]{1,0:T(8,128)}) %all-reduce.5.cloned.1.call-update) | async-done | bytes 3145744 | tf_op jit(solution)/shard_map/psum | solution.py:78
  963.0 3.8 copy.38
  (30 shorter events, 0.2 us)
Async XLA Ops:
  30.4 14.1 %copy-start.4 = (u32[256]{0:T(256)S(1)}, u32[256]{0:T(256)}, u32[]{:S(2)}) copy-start(u32[256]{0:T(256)} %constant.118) | copy-start | bytes 3076
  30.4 15.4 %copy-start.2 = (s32[48]{0:T(128)S(1)}, s32[48]{0:T(128)}, u32[]{:S(2)}) copy-start(s32[48]{0:T(128)} %param.9) | copy-start | bytes 580
  30.4 15.6 %copy-start.3 = (s32[48]{0:T(128)S(1)}, s32[48]{0:T(128)}, u32[]{:S(2)}) copy-start(s32[48]{0:T(128)} %param.8) | copy-start | bytes 580
  30.4 604.5 %copy-start.1 = (s32[256]{0:T(256)S(1)}, s32[256]{0:T(256)}, u32[]{:S(2)}) copy-start(s32[256]{0:T(256)} %param.10) | copy-start | bytes 3076
  30.4 617.5 %all-to-all-start = ((bf16[128,256,256]{2,1,0:T(8,128)(2,1)}), bf16[128,256,256]{2,1,0:T(8,128)(2,1)}, u32[]{:S(2)}, u32[]{:S(2)}) async-start(bf16[128,256,256]{2,1,0:T(8,128)(2,1)} %scatter_fusion.1), calls=%async_computation | async-start | bytes 33554432 | tf_op jit(solution)/shard_map/all_to_all | solution.py:76
  43.6 595.7 %copy-start = (s32[128,2]{1,0:T(8,128)S(1)}, s32[128,2]{1,0:T(8,128)}, u32[]{:S(2)}) copy-start(s32[128,2]{1,0:T(8,128)} %constant.110.clone.1) | copy-start | bytes 3076
  43.6 604.2 %all-gather.2.cloned.1.call-start = ((), (), s32[]{:S(2)}) async-start(), calls=%async_computation.1 | async-start | bytes 7864320 | tf_op jit(solution)/shard_map/all_gather | solution.py:73
  44.4 918.6 %all-reduce.5.cloned.1.call-start = ((), (), s32[]{:S(2)}) async-start(), calls=%async_computation.2 | async-start | bytes 6291456 | tf_op jit(solution)/shard_map/psum | solution.py:78
Sparse Core Ops, SparseCore 0:
  46.3 69.3 all-gather.1
  881.9 81.1 all-reduce.4
where the time goes:
time: 974 us
  blocking collectives  589 us (60%)
  matrix products  194 us (20%)
  waiting for transfers between devices  82 us (8%)
  local copies, waits for them, and re-layouts  78 us (8%)
  between operations  14.2 us (1%)
  starting transfers between devices  13.3 us (1%)
    unnamed x1, blocking collectives  589 us
    dot_general x4, matrix products, one_block(): jnp.einsum('sr,sac->rac', row_hits, products, precision=lax.Precision.HIG...  123 us
    psum x1, waiting for transfers between devices, per_device(): summed = lax.psum(summed, 'grp')  81.3 us
    dot_general x4, matrix products, one_block(): jnp.einsum('sab,sbc->sac', part_tiles, chosen, preferred_element_type=jnp...  70.7 us
    gather x4, local copies, waits for them, and re-layouts, one_block(): chosen = jnp.take(panel_tiles, part_labels[:, 1], axis=0)  37.2 us
  transfers between devices with their start and end apart: 3, of which 1 were waited for; matrix products, arithmetic and copies ran while one was open for 1% of the time, Pallas kernels for 0%

commit v1 on v0

--- a/solution.py
+++ b/solution.py
@@ -75,7 +75,9 @@
     summed = jnp.zeros((out_dev, tile_side, gathered.shape[1]), jnp.float32)
     arrived = lax.all_to_all(outgoing, "wide", split_axis=0, concat_axis=0, tiled=True)
     summed = add_products(summed, arrived, arrived_labels, panel_tiles)
-    summed = lax.psum(summed, "grp")
+    summed = summed
+    for hop in (1, 2):
+        summed = summed + lax.ppermute(summed, "grp", [(dev, dev ^ hop) for dev in range(4)])
     return summed.reshape(out_dev * tile_side, gathered.shape[1])
 
 

time: 974 us -> 1030 us (1.057)
  waiting for transfers between devices: 82 us -> 129 us
    ppermute x0 -> x2, waiting for transfers between devices: none -> 128 us  [per_device(): lax.ppermute(summed, 'grp', [(dev, dev ^ hop) for dev in range(4)])]
    psum x1 -> x0, waiting for transfers between devices: 81.3 us -> none  [per_device(): summed = lax.psum(summed, 'grp')]
  transfers between devices with their start and end apart: 3 -> 4, of which waited for: 1 -> 2; matrix products, arithmetic and copies ran while one was open for 1% -> 1% of each run, Pallas kernels for 0% -> 0%
where the time goes in v1:
time: 1030 us; the launch traced here: 1020 us
  blocking collectives  589 us (57%)
  matrix products  194 us (19%)
  waiting for transfers between devices  129 us (13%)
  local copies, waits for them, and re-layouts  74.2 us (7%)
  starting transfers between devices  17.3 us (2%)
  between operations  14.2 us (1%)
    unnamed x1, blocking collectives  589 us
    ppermute x2, waiting for transfers between devices, per_device(): lax.ppermute(summed, 'grp', [(dev, dev ^ hop) for dev in range(4)])  128 us
    dot_general x4, matrix products, one_block(): jnp.einsum('sr,sac->rac', row_hits, products, precision=lax.Precision.HIG...  123 us
    dot_general x4, matrix products, one_block(): jnp.einsum('sab,sbc->sac', part_tiles, chosen, preferred_element_type=jnp...  70.7 us
    gather x4, local copies, waits for them, and re-layouts, one_block(): chosen = jnp.take(panel_tiles, part_labels[:, 1], axis=0)  37.2 us
  transfers between devices with their start and end apart: 4, of which 2 were waited for; matrix products, arithmetic and copies ran while one was open for 1% of the time, Pallas kernels for 0%

profile of v1, /device:TPU:1, one launch (start us, length us, event | category | flops | bytes accessed | tf_op | source)
XLA Modules:
  0.0 1022.8 jit_solution(14549203700442681390)
XLA Ops:
  6.5 0.9 select_reduce_fusion.1
  7.4 0.2 convert_reduce_fusion.1
  7.6 5.9 broadcast_in_dim.68
  13.5 16.8 %scatter_fusion.1 = bf16[128,256,256]{2,1,0:T(8,128)(2,1)} fusion(bf16[128,256,256]{2,1,0:T(8,128)(2,1)} %broadcast_in_dim.68, s32[48]{0:T(128)S(1)} %fusion.19, bf16[48,256,256]{2,1,0:T(8,128)(2,1)} %param.7), kind=kCustom, calls=%fused_computation.2 | custom fusion | bytes 18874560 | tf_op jit(solution)/shard_map/scatter | solution.py:55
  30.4 13.3 %all-to-all-start = ((bf16[128,256,256]{2,1,0:T(8,128)(2,1)}), bf16[128,256,256]{2,1,0:T(8,128)(2,1)}, u32[]{:S(2)}, u32[]{:S(2)}) async-start(bf16[128,256,256]{2,1,0:T(8,128)(2,1)} %scatter_fusion.1), calls=%async_computation | async-start | bytes 33554432 | tf_op jit(solution)/shard_map/all_to_all | solution.py:76
  43.6 0.0 copy-start
  43.6 0.0 all-gather.2.cloned.1.call-start
  43.7 0.7 all-gather.2.cloned.1.call-update
  44.4 0.6 dynamic-slice
  45.7 0.3 dynamic-update-slice
  46.0 0.3 dynamic-update-slice.1
  46.2 588.6 %all-reduce.2 = (s32[3072]{0:T(1024)S(1)}, s32[3072]{0:T(1024)S(1)}) all-reduce(s32[3072]{0:T(1024)S(1)} %dynamic-update-slice, s32[3072]{0:T(1024)S(1)} %dynamic-update-slice.1), channel_id=1, replica_groups=mesh['grp'=4,'wide'=64] {'wide'}, use_global_device_ids=true, to_apply=%add | all-reduce | flops 6144 | bytes 49152
  634.8 0.1 eq.107
  634.9 1.7 select_reduce_fusion
  636.6 0.1 reduce_sum.43
  636.7 0.1 copy.11
  636.8 0.5 convert_reduce_fusion
  637.3 0.1 copy.13
  637.4 0.1 add.156
  637.5 0.1 and_select_fusion
  637.6 1.7 copy.14
  639.3 8.5 scatter_fusion
  647.8 0.1 copy.15
  647.9 0.0 all-to-all-done
  647.9 231.8 %while.14 = (s32[]{:T(128)}, f32[4,256,768]{2,0,1:T(4,128)S(1)}, s32[128,2]{0,1:T(2,128)S(1)}, bf16[128,256,256]{2,1,0:T(8,128)(2,1)}, bf16[16,256,768]{2,1,0:T(...) while((s32[]{:T(128)}, f32[4,256,768]{2,0,1:T(4,128)S(1)}, ...), condition=%wide.region_7.8_spmd.clone, body=%wide.region_6.7_spmd.clone.sunk | while | flops 3531081216 | bytes 98572000 | solution.py:38
  648.1 0.1 constant_dynamic-slice_fusion.2
  648.2 9.4 gather_fusion
  657.5 17.7 %fusion.29 = f32[32,256,768]{2,1,0:T(8,128)} fusion(bf16[32,256,768]{2,1,0:T(8,128)(2,1)} %gather_fusion, pred[32]{0:T(512)(128)(4,1)S(1)} %and_bitcast_fusion.2, bf16[128,256,256]{2,1,0:T(8,128)(2,1)} %get-tuple-element.217, s32[]{:T(128)S(6)} %select_n.171), kind=kOutput, calls=%fused_computation.6.clone.1 | convolution fusion | flops 3227516928 | bytes 41943076 | tf_op jit(solution)/shard_map/while/body/eval_jaxpr/sab,sbc->sac/dot_general | solution.py:30
  675.2 30.7 %select_add_fusion.2 = f32[4,256,768]{2,0,1:T(4,128)S(1)} fusion(f32[4,256,768]{2,0,1:T(4,128)S(1)} %get-tuple-element.206, pred[]{:T(512)S(6)} %compare.49, f32[32,256,768]{2,1,0:T(8,128)} %fusion.29, s32[32]{0:T(128)S(1)} %get-tuple-element.195), kind=kOutput, calls=%fused_computation.11.clone.1 | convolution fusion | flops 303562880 | bytes 31457408 | tf_op jit(solution)/shard_map/while/body/eval_jaxpr/sr,sac->rac/dot_general | solution.py:34
  706.0 0.1 constant_dynamic-slice_fusion.2
  706.1 9.3 gather_fusion
  715.4 17.7 %fusion.29 = f32[32,256,768]{2,1,0:T(8,128)} fusion(bf16[32,256,768]{2,1,0:T(8,128)(2,1)} %gather_fusion, pred[32]{0:T(512)(128)(4,1)S(1)} %and_bitcast_fusion.2, bf16[128,256,256]{2,1,0:T(8,128)(2,1)} %get-tuple-element.217, s32[]{:T(128)S(6)} %select_n.171), kind=kOutput, calls=%fused_computation.6.clone.1 | convolution fusion | flops 3227516928 | bytes 41943076 | tf_op jit(solution)/shard_map/while/body/eval_jaxpr/sab,sbc->sac/dot_general | solution.py:30
  733.1 30.7 %select_add_fusion.2 = f32[4,256,768]{2,0,1:T(4,128)S(1)} fusion(f32[4,256,768]{2,0,1:T(4,128)S(1)} %get-tuple-element.206, pred[]{:T(512)S(6)} %compare.49, f32[32,256,768]{2,1,0:T(8,128)} %fusion.29, s32[32]{0:T(128)S(1)} %get-tuple-element.195), kind=kOutput, calls=%fused_computation.11.clone.1 | convolution fusion | flops 303562880 | bytes 31457408 | tf_op jit(solution)/shard_map/while/body/eval_jaxpr/sr,sac->rac/dot_general | solution.py:34
  763.8 0.1 constant_dynamic-slice_fusion.2
  763.9 9.3 gather_fusion
  773.2 17.7 %fusion.29 = f32[32,256,768]{2,1,0:T(8,128)} fusion(bf16[32,256,768]{2,1,0:T(8,128)(2,1)} %gather_fusion, pred[32]{0:T(512)(128)(4,1)S(1)} %and_bitcast_fusion.2, bf16[128,256,256]{2,1,0:T(8,128)(2,1)} %get-tuple-element.217, s32[]{:T(128)S(6)} %select_n.171), kind=kOutput, calls=%fused_computation.6.clone.1 | convolution fusion | flops 3227516928 | bytes 41943076 | tf_op jit(solution)/shard_map/while/body/eval_jaxpr/sab,sbc->sac/dot_general | solution.py:30
  790.9 30.7 %select_add_fusion.2 = f32[4,256,768]{2,0,1:T(4,128)S(1)} fusion(f32[4,256,768]{2,0,1:T(4,128)S(1)} %get-tuple-element.206, pred[]{:T(512)S(6)} %compare.49, f32[32,256,768]{2,1,0:T(8,128)} %fusion.29, s32[32]{0:T(128)S(1)} %get-tuple-element.195), kind=kOutput, calls=%fused_computation.11.clone.1 | convolution fusion | flops 303562880 | bytes 31457408 | tf_op jit(solution)/shard_map/while/body/eval_jaxpr/sr,sac->rac/dot_general | solution.py:34
  821.7 0.1 constant_dynamic-slice_fusion.2
  821.8 9.2 gather_fusion
  831.0 17.7 %fusion.29 = f32[32,256,768]{2,1,0:T(8,128)} fusion(bf16[32,256,768]{2,1,0:T(8,128)(2,1)} %gather_fusion, pred[32]{0:T(512)(128)(4,1)S(1)} %and_bitcast_fusion.2, bf16[128,256,256]{2,1,0:T(8,128)(2,1)} %get-tuple-element.217, s32[]{:T(128)S(6)} %select_n.171), kind=kOutput, calls=%fused_computation.6.clone.1 | convolution fusion | flops 3227516928 | bytes 41943076 | tf_op jit(solution)/shard_map/while/body/eval_jaxpr/sab,sbc->sac/dot_general | solution.py:30
  848.7 30.7 %select_add_fusion.2 = f32[4,256,768]{2,0,1:T(4,128)S(1)} fusion(f32[4,256,768]{2,0,1:T(4,128)S(1)} %get-tuple-element.206, pred[]{:T(512)S(6)} %compare.49, f32[32,256,768]{2,1,0:T(8,128)} %fusion.29, s32[32]{0:T(128)S(1)} %get-tuple-element.195), kind=kOutput, calls=%fused_computation.11.clone.1 | convolution fusion | flops 303562880 | bytes 31457408 | tf_op jit(solution)/shard_map/while/body/eval_jaxpr/sr,sac->rac/dot_general | solution.py:34
  879.7 1.0 collective-permute-start
  880.7 62.2 %collective-permute-done = f32[4,256,768]{2,0,1:T(4,128)S(1)} collective-permute-done((f32[4,256,768]{2,0,1:T(4,128)S(1)}, f32[4,256,768]{2,0,1:T(4,128)S(1)}, u32[]{:S(2)}, u32[]{:S(2)}) %collective-permute-start) | collective-permute-done | bytes 3145760 | tf_op jit(solution)/shard_map/ppermute | solution.py:80
  943.0 0.8 add.162
  943.8 3.0 collective-permute-start.1
  946.8 66.2 %collective-permute-done.1 = f32[4,256,768]{2,0,1:T(4,128)S(1)} collective-permute-done((f32[4,256,768]{2,0,1:T(4,128)S(1)}, f32[4,256,768]{2,0,1:T(4,128)S(1)}, u32[]{:S(2)}, u32[]{:S(2)}) %collective-permute-start.1) | collective-permute-done | bytes 3145760 | tf_op jit(solution)/shard_map/ppermute | solution.py:80
  1012.9 0.8 add.163
  1013.7 2.2 copy.16
  (32 shorter events, 0.2 us)
Async XLA Ops:
  30.4 14.1 %copy-start.4 = (u32[256]{0:T(256)S(1)}, u32[256]{0:T(256)}, u32[]{:S(2)}) copy-start(u32[256]{0:T(256)} %constant.118) | copy-start | bytes 3076
  30.4 15.3 %copy-start.2 = (s32[48]{0:T(128)S(1)}, s32[48]{0:T(128)}, u32[]{:S(2)}) copy-start(s32[48]{0:T(128)} %param.9) | copy-start | bytes 580
  30.4 15.6 %copy-start.3 = (s32[48]{0:T(128)S(1)}, s32[48]{0:T(128)}, u32[]{:S(2)}) copy-start(s32[48]{0:T(128)} %param.8) | copy-start | bytes 580
  30.4 604.5 %copy-start.1 = (s32[256]{0:T(256)S(1)}, s32[256]{0:T(256)}, u32[]{:S(2)}) copy-start(s32[256]{0:T(256)} %param.10) | copy-start | bytes 3076
  30.4 617.5 %all-to-all-start = ((bf16[128,256,256]{2,1,0:T(8,128)(2,1)}), bf16[128,256,256]{2,1,0:T(8,128)(2,1)}, u32[]{:S(2)}, u32[]{:S(2)}) async-start(bf16[128,256,256]{2,1,0:T(8,128)(2,1)} %scatter_fusion.1), calls=%async_computation | async-start | bytes 33554432 | tf_op jit(solution)/shard_map/all_to_all | solution.py:76
  43.6 595.7 %copy-start = (s32[128,2]{1,0:T(8,128)S(1)}, s32[128,2]{1,0:T(8,128)}, u32[]{:S(2)}) copy-start(s32[128,2]{1,0:T(8,128)} %constant.110.clone.1) | copy-start | bytes 3076
  43.6 604.2 %all-gather.2.cloned.1.call-start = ((), (), s32[]{:S(2)}) async-start(), calls=%async_computation.1 | async-start | bytes 7864320 | tf_op jit(solution)/shard_map/all_gather | solution.py:73
  879.7 63.3 %collective-permute-start = (f32[4,256,768]{2,0,1:T(4,128)S(1)}, f32[4,256,768]{2,0,1:T(4,128)S(1)}, u32[]{:S(2)}, u32[]{:S(2)}) collective-permute-start(f32[4,256,768]{2,0,1:T(4,128)S(1)} %get-tuple-element.114), channel_id=1, source_target_pairs={{0,64},{64,0},{128,192},{192,128},{1,65},{65,1},{129,193},{193,129... | collective-permute-start | bytes 9437192 | tf_op jit(solution)/shard_map/ppermute | solution.py:80
  943.8 69.1 %collective-permute-start.1 = (f32[4,256,768]{2,0,1:T(4,128)S(1)}, f32[4,256,768]{2,0,1:T(4,128)S(1)}, u32[]{:S(2)}, u32[]{:S(2)}) collective-permute-start(f32[4,256,768]{2,0,1:T(4,128)S(1)} %add.162), channel_id=1, source_target_pairs={{0,128},{64,192},{128,0},{192,64},{1,129},{65,193},{129,1},{193,65... | collective-permute-start | bytes 9437192 | tf_op jit(solution)/shard_map/ppermute | solution.py:80
Sparse Core Ops, SparseCore 0:
  46.3 69.3 all-gather.1
